TPU v7x, 512 devices: a whole 4x8x8 slice. The times are simulated.
512 devices in a mesh: tok: 16 (over y, core), voc: 32 (over x, z).
Axes of the slice: x: 4, y: 8, z: 8, core: 2. Of those that a mesh axis runs over, the one named last changes fastest.
Arguments:
- hidden: bfloat16 [4096, 2048], P('tok')
- panel: bfloat16 [2048, 8192], P(None, 'voc'), may hold values from -0.25 to 0.25
- in_proj: bfloat16 [2048, 64], replicated, may hold values from -0.125 to 0.125
- out_proj: bfloat16 [8192, 64], P('voc'), may hold values from -6 to 6
- targets: int32 [4096], P('tok'), may hold values from 0 to 8191
- keep: int32 [4096], P('tok'), may hold values 0 or 1
- span_ids: int32 [4096], P('tok'), may hold values from 0 to 511, as said below
- store: bfloat16 [131072, 4096], P(('tok', 'voc')), may hold values from -6 to 6
Outputs:
- hidden_grad: bfloat16 [4096, 2048], P('tok', 'voc')
- scores: float32 [512, 131072], P(None, ('tok', 'voc'))
Inputs may be any that keep to these rules, and one draw needn't show every extreme that they name: `span_ids`: tokens k * 256 to (k + 1) * 256 - 1 hold exactly the spans k * 32 to (k + 1) * 32 - 1 in increasing order, each of one or more tokens.
All inputs are finite; a program needn't handle non-finite values. No bound on the sum of `keep` on one device may be relied on, other than what follows from the above.
Results may differ from a plain program's by a relative error of at most 0.018.
Values may be sent and summed in bfloat16 or wider, within the bound.
No kernel may reach another device: no remote copies, remote signals or barrier semaphores. Data moves between devices by JAX's collectives and lax.ppermute only.
A program may use at most 64 MiB of HBM per device.

v0:
```python
import jax
import jax.numpy as jnp
from jax import lax
from jax.sharding import PartitionSpec as P

RANK = 64
SPAN_DEV = 32


def sent_to_all(array, axis):
    devices = lax.axis_size(axis)
    return lax.all_to_all(
        jnp.broadcast_to(array[None], (devices, *array.shape)), axis, 0, 0, tiled=True
    )


def collected_together(array, axis):
    leaves = jax.tree.leaves(array)
    order = sorted(range(len(leaves)), key=lambda k: -leaves[k].size)
    width = (1, *leaves[order[0]].shape)[-1]
    lines = [
        jnp.pad(leaves[k].reshape(-1), (0, -leaves[k].size % width)).reshape(-1, width)
        for k in order
    ]
    both, at, found = (sent_to_all(jnp.concatenate(lines), axis), 0, {})
    for k, line in zip(order, lines):
        share = both[:, at : at + len(line)].reshape(len(both), -1)
        found[k] = share[:, : leaves[k].size].reshape(-1, *leaves[k].shape)
        at += len(line)
    numbers = iter(range(len(leaves)))
    return jax.tree.map(lambda _: found[next(numbers)], array)


def combined_pairwise(pieces, combine):
    while len(jax.tree.leaves(pieces)[0]) > 1:
        pieces = jax.vmap(combine)(
            *(jax.tree.map(lambda part: part[side::2], pieces) for side in (0, 1))
        )
    return jax.tree.map(lambda part: part[0], pieces)


def merged(array, axis, combine):
    pieces = collected_together(array, axis)
    return combined_pairwise(pieces, combine)


def in_blocks(array, dim, devices):
    lengths = array.shape
    parts = array.reshape(*lengths[:dim], devices, lengths[dim] // devices, *lengths[dim + 1 :])
    return jnp.moveaxis(parts, dim, 0)


def sum_at_owner(array, axis, dim):
    devices = lax.axis_size(axis)
    parts = lax.all_to_all(in_blocks(array, dim, devices), axis, 0, 0, tiled=True)
    return jnp.sum(parts.astype(jnp.float32), axis=0)


def of_everyone(array, axis):
    everything = sent_to_all(array, axis)
    return jnp.sum(everything.astype(jnp.float32), axis=0)


def combine_stats(first, second):
    top = jnp.maximum(first[0], second[0])
    total = first[1] * jnp.exp(first[0] - top) + second[1] * jnp.exp(second[0] - top)
    return (top, total)


def span_sums(member, inner, outer):
    weighted = member[:, :, None] * inner[None, :, :]
    summed = lax.dot_general(
        weighted,
        outer,
        (((1,), (0,)), ((), ())),
        precision=lax.Precision.HIGHEST,
        preferred_element_type=jnp.float32,
    )
    return summed.reshape(member.shape[0], inner.shape[1] * outer.shape[1])


def body(hidden, panel, in_proj, out_proj, targets, keep, span_ids, store):
    panel_cols = panel.shape[1]
    logits = jnp.dot(hidden, panel, preferred_element_type=jnp.float32)
    local_top = jnp.max(logits, axis=1)
    local_total = jnp.sum(jnp.exp(logits - local_top[:, None]), axis=1)
    top, total = merged((local_top, local_total), "voc", combine_stats)
    lse = top + jnp.log(total)
    columns = lax.axis_index("voc") * panel_cols + jnp.arange(panel_cols, dtype=jnp.int32)
    onehot = (targets[:, None] == columns[None, :]).astype(jnp.float32)
    grad = ((jnp.exp(logits - lse[:, None]) - onehot) * keep.astype(jnp.float32)[:, None]).astype(
        jnp.bfloat16
    )
    partial_hidden = lax.dot_general(
        grad, panel, (((1,), (1,)), ((), ())), preferred_element_type=jnp.float32
    )
    hidden_grad = sum_at_owner(partial_hidden.astype(jnp.bfloat16), "voc", 1).astype(jnp.bfloat16)
    inner = jnp.dot(hidden, in_proj, preferred_element_type=jnp.float32)
    outer_part = jnp.dot(grad, out_proj, preferred_element_type=jnp.float32)
    local_span = span_ids - lax.axis_index("tok") * SPAN_DEV
    member = (local_span[None, :] == jnp.arange(SPAN_DEV, dtype=jnp.int32)[:, None]).astype(
        jnp.float32
    )
    outer = of_everyone(outer_part.astype(jnp.bfloat16), "voc").astype(jnp.float32)
    queries = span_sums(member, inner, outer).astype(jnp.bfloat16)
    scores = (
        lax.dot_general(
            lax.all_gather(queries, "tok", axis=0, tiled=True),
            store,
            (((1,), (1,)), ((), ())),
            preferred_element_type=jnp.float32,
        )
        / RANK
    )
    return (hidden_grad, scores)


def solution(mesh):
    placed = (
        P("tok", None),
        P(None, "voc"),
        P(),
        P("voc", None),
        P("tok"),
        P("tok"),
        P("tok"),
        P(("tok", "voc"), None),
    )
    return jax.shard_map(
        body,
        mesh=mesh,
        in_specs=placed,
        out_specs=(P("tok", "voc"), P(None, ("tok", "voc"))),
        check_vma=False,
    )
```

profile of v0, /device:TPU:1, one launch (start us, length us, event | category | flops | bytes accessed | tf_op | source)
XLA Modules:
  0.0 127.9 jit_solution(8398585282720557890)
XLA Ops:
  7.2 0.0 copy-start
  7.2 0.0 copy-start.4
  7.2 0.0 copy-start.3
  7.2 2.2 %fusion.12 = (f32[256]{0:T(256)S(1)}, f32[256,256]{0,1:T(8,128)S(1)}) fusion(bf16[256,2048]{1,0:T(8,128)(2,1)} %param.8, bf16[2048,256]{1,0:T(8,128)(2,1)} %param.9), kind=kOutput, calls=%fused_computation.30 | convolution fusion | flops 268500736 | bytes 2360320 | tf_op jit(solution)/shard_map/dot_general | solution.py:84
  9.4 0.1 exponential_reduce_fusion
  9.5 0.7 broadcast_in_dim.4
  10.2 13.7 %all-to-all-start = ((f32[32,2,256]{2,1,0:T(2,128)}), f32[32,2,256]{2,1,0:T(2,128)S(1)}, u32[]{:S(2)}, u32[]{:S(2)}) async-start(f32[32,2,256]{2,1,0:T(2,128)} %broadcast_in_dim.4), calls=%async_computation | async-start | bytes 131072 | tf_op jit(solution)/shard_map/all_to_all | solution.py:12
  23.9 0.0 copy-done.4
  23.9 8.8 %all-to-all-done = f32[32,2,256]{2,1,0:T(2,128)S(1)} async-done(((f32[32,2,256]{2,1,0:T(2,128)}), f32[32,2,256]{2,1,0:T(2,128)S(1)}, u32[]{:S(2)}, u32[]{:S(2)}) %all-to-all-start) | async-done | bytes 65568 | tf_op jit(solution)/shard_map/all_to_all | solution.py:12
  32.7 0.1 fusion.11
  32.8 0.0 copy-start.5
  32.8 0.0 copy-start.1
  33.2 0.0 copy-done.3
  33.3 1.0 convolution_convert_fusion.1
  34.2 1.2 broadcast_in_dim.5
  35.4 4.7 %all-to-all-start.2 = ((bf16[32,256,64]{1,2,0:T(8,128)(2,1)}), bf16[32,256,64]{1,2,0:T(8,128)(2,1)}, u32[]{:S(2)}, u32[]{:S(2)}) async-start(bf16[32,256,64]{1,2,0:T(8,128)(2,1)} %broadcast_in_dim.5), calls=%async_computation.2 | async-start | bytes 2097152 | tf_op jit(solution)/shard_map/all_to_all | solution.py:12
  40.1 0.0 all-gather.2.cloned.1.call-start
  40.1 0.0 copy-done.5
  40.2 0.0 copy-done.1
  40.2 1.4 %fusion.13 = f32[256,64]{0,1:T(8,128)S(1)} fusion(bf16[256,2048]{1,0:T(8,128)(2,1)S(1)} %copy-done.1, bf16[2048,64]{0,1:T(8,128)(2,1)} %param.10), kind=kOutput, calls=%fused_computation.31 | convolution fusion | flops 67108864 | bytes 1376256 | tf_op jit(solution)/shard_map/dot_general | solution.py:98
  41.6 0.0 copy-start.2
  41.6 22.9 %all-to-all-done.2 = bf16[32,256,64]{1,2,0:T(8,128)(2,1)} async-done(((bf16[32,256,64]{1,2,0:T(8,128)(2,1)}), bf16[32,256,64]{1,2,0:T(8,128)(2,1)}, u32[]{:S(2)}, u32[]{:S(2)}) %all-to-all-start.2) | async-done | bytes 1048608 | tf_op jit(solution)/shard_map/all_to_all | solution.py:12
  64.5 1.4 %convert_reduce_fusion = f32[256,64]{0,1:T(8,128)S(1)} fusion(bf16[32,256,64]{1,2,0:T(8,128)(2,1)} %all-to-all-done.2), kind=kLoop, calls=%fused_computation.1 | loop fusion | flops 1032192 | bytes 1114112 | tf_op jit(solution)/shard_map/reduce_sum | solution.py:61
  65.9 2.6 %fusion.2 = bf16[32,64,64]{2,1,0:T(8,128)(2,1)} fusion(f32[256,64]{0,1:T(8,128)S(1)} %fusion.13, f32[32,256]{1,0:T(8,128)S(1)} %fusion.8, f32[256,64]{0,1:T(8,128)S(1)} %convert_reduce_fusion), kind=kOutput, calls=%fused_computation.4 | convolution fusion | flops 403308544 | bytes 425984 | tf_op jit(solution)/shard_map/dot_general | solution.py:72
  68.5 2.2 %convert_element_type.41 = bf16[32,4096]{1,0:T(8,128)(2,1)} reshape(bf16[32,64,64]{2,1,0:T(8,128)(2,1)} %fusion.2) | data formatting | bytes 524288 | tf_op jit(solution)/shard_map/convert_element_type | solution.py:105
  70.7 0.0 all-gather.2.cloned.1.call-update
  70.7 1.5 %convolution_convert_fusion = bf16[256,2048]{1,0:T(8,128)(2,1)} fusion(bf16[2048,256]{1,0:T(8,128)(2,1)S(1)} %copy-done.2, f32[256,256]{0,1:T(8,128)S(1)} %get-tuple-element.13, f32[256]{0:T(256)S(1)} %convert_element_type.34, s32[256]{0:T(256)S(1)} %copy-done.3, f32[256]{0:T(256)S(1)} %bitcast.24, s32[256]{0:T(256)S(1)} %iota_add_fusion), kind=kOutput, calls=%fused_computation | convolution fusion | flops 269352960 | bytes 2363392 | tf_op jit(solution)/shard_map/dot_general | solution.py:94
  72.3 2.3 %copy.14 = bf16[256,2048]{0,1:T(8,128)(2,1)} copy(bf16[256,2048]{1,0:T(8,128)(2,1)} %convolution_convert_fusion) | data formatting | bytes 2097152 | tf_op jit(solution)/shard_map/convert_element_type | solution.py:97
  74.5 32.7 %all_to_all.15 = bf16[32,256,64]{1,2,0:T(8,128)(2,1)S(1)} all-to-all(bf16[32,256,64]{1,2,0:T(8,128)(2,1)} %bitcast.21), channel_id=1, replica_groups=mesh['tok'=16,'voc'=32] {'voc'}, dimensions={0} | all-to-all | bytes 2097152 | tf_op jit(solution)/shard_map/all_to_all | solution.py:55
  107.2 0.8 reduce_sum.31
  108.0 8.8 %all-gather.2.cloned.1.call-done = bf16[512,4096]{1,0:T(8,128)(2,1)} async-done(((bf16[32,4096]{1,0:T(8,128)(2,1)}), bf16[512,4096]{1,0:T(8,128)(2,1)}) %all-gather.2.cloned.1.call-update) | async-done | bytes 4194320 | tf_op jit(solution)/shard_map/all_gather | solution.py:108
  116.8 4.3 %convolution_multiply_fusion = f32[512,256]{1,0:T(8,128)} fusion(bf16[512,4096]{1,0:T(8,128)(2,1)} %all-gather.2.cloned.1.call-done, bf16[256,4096]{1,0:T(8,128)(2,1)S(1)} %copy-done), kind=kOutput, calls=%fused_computation.5 | convolution fusion | flops 1073872896 | bytes 6815744 | tf_op jit(solution)/shard_map/dot_general | solution.py:107
  (29 shorter events, 0.4 us)
Async XLA Ops:
  7.2 109.6 %copy-start = (bf16[256,4096]{1,0:T(8,128)(2,1)S(1)}, bf16[256,4096]{1,0:T(8,128)(2,1)}, u32[]{:S(2)}) copy-start(bf16[256,4096]{1,0:T(8,128)(2,1)} %param.15) | copy-start | bytes 6291460
  7.2 16.7 %copy-start.4 = (s32[256]{0:T(256)S(1)}, s32[256]{0:T(256)}, u32[]{:S(2)}) copy-start(s32[256]{0:T(256)} %param.13) | copy-start | bytes 3076
  7.2 26.1 %copy-start.3 = (s32[256]{0:T(256)S(1)}, s32[256]{0:T(256)}, u32[]{:S(2)}) copy-start(s32[256]{0:T(256)} %param.12) | copy-start | bytes 3076
  10.2 22.6 %all-to-all-start = ((f32[32,2,256]{2,1,0:T(2,128)}), f32[32,2,256]{2,1,0:T(2,128)S(1)}, u32[]{:S(2)}, u32[]{:S(2)}) async-start(f32[32,2,256]{2,1,0:T(2,128)} %broadcast_in_dim.4), calls=%async_computation | async-start | bytes 131072 | tf_op jit(solution)/shard_map/all_to_all | solution.py:12
  32.8 7.3 %copy-start.5 = (s32[256]{0:T(256)S(1)}, s32[256]{0:T(256)}, u32[]{:S(2)}) copy-start(s32[256]{0:T(256)} %param.14) | copy-start | bytes 3076
  32.8 7.4 %copy-start.1 = (bf16[256,2048]{1,0:T(8,128)(2,1)S(1)}, bf16[256,2048]{1,0:T(8,128)(2,1)}, u32[]{:S(2)}) copy-start(bf16[256,2048]{1,0:T(8,128)(2,1)} %param.8) | copy-start | bytes 3145732
  35.4 29.1 %all-to-all-start.2 = ((bf16[32,256,64]{1,2,0:T(8,128)(2,1)}), bf16[32,256,64]{1,2,0:T(8,128)(2,1)}, u32[]{:S(2)}, u32[]{:S(2)}) async-start(bf16[32,256,64]{1,2,0:T(8,128)(2,1)} %broadcast_in_dim.5), calls=%async_computation.2 | async-start | bytes 2097152 | tf_op jit(solution)/shard_map/all_to_all | solution.py:12
  40.1 76.7 %all-gather.2.cloned.1.call-start = ((), (), s32[]{:S(2)}) async-start(), calls=%async_computation.3 | async-start | bytes 4456448 | tf_op jit(solution)/shard_map/all_gather | solution.py:108
  41.6 29.1 %copy-start.2 = (bf16[2048,256]{1,0:T(8,128)(2,1)S(1)}, bf16[2048,256]{1,0:T(8,128)(2,1)}, u32[]{:S(2)}) copy-start(bf16[2048,256]{1,0:T(8,128)(2,1)} %param.9) | copy-start | bytes 3145732
Sparse Core Ops, SparseCore 0:
  70.8 45.9 all-gather.1
where the time goes:
time: 128 us
  waiting for transfers between devices  40.6 us (32%)
  blocking collectives  32.7 us (26%)
  starting transfers between devices  18.4 us (14%)
  between operations  14.2 us (11%)
  matrix products  13 us (10%)
  local copies, waits for them, and re-layouts  6.66 us (5%)
  other arithmetic  2.33 us (2%)
    all_to_all x1, blocking collectives, sum_at_owner(): lax.all_to_all(in_blocks(array, dim, devices), axis, 0, 0, tiled=True)  32.7 us
    all_to_all x2, waiting for transfers between devices, sent_to_all(): lax.all_to_all(jnp.broadcast_to(array[None], (devices, *array.shape)), ax...  31.8 us
    all_to_all x2, starting transfers between devices, sent_to_all(): lax.all_to_all(jnp.broadcast_to(array[None], (devices, *array.shape)), ax...  18.4 us
    all_gather x1, waiting for transfers between devices, body(): lax.all_gather(queries, 'tok', axis=0, tiled=True)  8.82 us
    dot_general x1, matrix products, body(): lax.dot_general(lax.all_gather(queries, 'tok', axis=0, tiled=True), store...  4.26 us
    dot_general x1, matrix products, span_sums(): lax.dot_general(weighted, outer, (((1,), (0,)), ((), ())), precision=lax....  2.58 us
  transfers between devices with their start and end apart: 3, of which 3 were waited for; matrix products, arithmetic and copies ran while one was open for 5% of the time, Pallas kernels for 0%

commit v1 on v0

--- a/solution.py
+++ b/solution.py
@@ -5,6 +5,24 @@
 
 RANK = 64
 SPAN_DEV = 32
+
+
+def collect(value, axis, dim):
+    ways, here, step = (lax.axis_size(axis), lax.axis_index(axis), value.shape[dim])
+    shape = [n * ways if d == dim else n for d, n in enumerate(value.shape)]
+    full = lax.dynamic_update_slice_in_dim(
+        jnp.zeros(shape, value.dtype), value, here * step, axis=dim
+    )
+    going_up = going_down = value
+    for far in range(1, ways // 2 + 1):
+        going_up = lax.ppermute(going_up, axis, [(d, (d + 1) % ways) for d in range(ways)])
+        full = lax.dynamic_update_slice_in_dim(full, going_up, (here - far) % ways * step, axis=dim)
+        if 2 * far < ways:
+            going_down = lax.ppermute(going_down, axis, [(d, (d - 1) % ways) for d in range(ways)])
+            full = lax.dynamic_update_slice_in_dim(
+                full, going_down, (here + far) % ways * step, axis=dim
+            )
+    return full
 
 
 def sent_to_all(array, axis):
@@ -105,7 +123,7 @@
     queries = span_sums(member, inner, outer).astype(jnp.bfloat16)
     scores = (
         lax.dot_general(
-            lax.all_gather(queries, "tok", axis=0, tiled=True),
+            collect(queries, "tok", 0),
             store,
             (((1,), (1,)), ((), ())),
             preferred_element_type=jnp.float32,

time: 128 us -> 149 us (1.16)
  the two profiles are of different devices: /device:TPU:1 before, /device:TPU:32 now
where the time goes in v1:
time: 149 us; the launch traced here: 148 us
  waiting for transfers between devices  84 us (56%)
  starting transfers between devices  43.8 us (29%)
  matrix products  9.08 us (6%)
  local copies, waits for them, and re-layouts  5.86 us (4%)
  other arithmetic  4.26 us (3%)
    all_to_all x2, waiting for transfers between devices, sent_to_all(): lax.all_to_all(jnp.broadcast_to(array[None], (devices, *array.shape)), ax...  32.9 us
    ppermute x8, waiting for transfers between devices, collect(): lax.ppermute(going_up, axis, [(d, (d + 1) % ways) for d in range(ways)])  30.9 us
    ppermute x7, starting transfers between devices, collect(): lax.ppermute(going_down, axis, [(d, (d - 1) % ways) for d in range(ways)])  20.7 us
    all_to_all x1, waiting for transfers between devices, sum_at_owner(): lax.all_to_all(in_blocks(array, dim, devices), axis, 0, 0, tiled=True)  20.2 us
    all_to_all x2, starting transfers between devices, sent_to_all(): lax.all_to_all(jnp.broadcast_to(array[None], (devices, *array.shape)), ax...  18 us
    all_to_all x1, starting transfers between devices, sum_at_owner(): lax.all_to_all(in_blocks(array, dim, devices), axis, 0, 0, tiled=True)  5.15 us
  transfers between devices with their start and end apart: 18, of which 10 were waited for; matrix products, arithmetic and copies ran while one was open for 8% of the time, Pallas kernels for 0%

profile of v1, /device:TPU:32, one launch (start us, length us, event | category | flops | bytes accessed | tf_op | source)
XLA Modules:
  0.0 148.2 jit_solution(12002320994797001017)
XLA Ops:
  0.7 2.2 %fusion.12 = (f32[256]{0:T(256)S(1)}, f32[256,256]{0,1:T(8,128)S(1)}) fusion(bf16[256,2048]{1,0:T(8,128)(2,1)} %param.8, bf16[2048,256]{1,0:T(8,128)(2,1)} %param.9), kind=kOutput, calls=%fused_computation.46 | convolution fusion | flops 268500736 | bytes 2360320 | tf_op jit(solution)/shard_map/dot_general | solution.py:102
  3.0 0.7 broadcast_in_dim.6
  3.6 13.2 %all-to-all-start = ((f32[32,2,256]{2,1,0:T(2,128)}), f32[32,2,256]{2,1,0:T(2,128)S(1)}, u32[]{:S(2)}, u32[]{:S(2)}) async-start(f32[32,2,256]{2,1,0:T(2,128)} %broadcast_in_dim.6), calls=%async_computation | async-start | bytes 131072 | tf_op jit(solution)/shard_map/all_to_all | solution.py:30
  16.8 0.7 convert_element_type.34
  17.5 9.3 %all-to-all-done = f32[32,2,256]{2,1,0:T(2,128)S(1)} async-done(((f32[32,2,256]{2,1,0:T(2,128)}), f32[32,2,256]{2,1,0:T(2,128)S(1)}, u32[]{:S(2)}, u32[]{:S(2)}) %all-to-all-start) | async-done | bytes 65568 | tf_op jit(solution)/shard_map/all_to_all | solution.py:30
  27.3 1.0 convolution_convert_fusion.1
  28.3 1.1 broadcast_in_dim.8
  29.4 4.8 %all-to-all-start.2 = ((bf16[32,256,64]{1,2,0:T(8,128)(2,1)}), bf16[32,256,64]{1,2,0:T(8,128)(2,1)}, u32[]{:S(2)}, u32[]{:S(2)}) async-start(bf16[32,256,64]{1,2,0:T(8,128)(2,1)} %broadcast_in_dim.8), calls=%async_computation.2 | async-start | bytes 2097152 | tf_op jit(solution)/shard_map/all_to_all | solution.py:30
  34.2 1.6 %convolution_convert_fusion = bf16[256,2048]{1,0:T(8,128)(2,1)} fusion(bf16[2048,256]{1,0:T(8,128)(2,1)S(1)} %copy-done.1, f32[256,256]{0,1:T(8,128)S(1)} %get-tuple-element.13, f32[256]{0:T(256)S(1)} %convert_element_type.34, s32[256]{0:T(256)S(1)} %copy-done.4, f32[256]{0:T(256)S(1)} %bitcast.24, s32[256]{0:T(256)S(1)} %iota_add_fusion), kind=kOutput, calls=%fused_computation | convolution fusion | flops 269352960 | bytes 2363392 | tf_op jit(solution)/shard_map/dot_general | solution.py:112
  35.8 2.4 %copy.14 = bf16[256,2048]{0,1:T(8,128)(2,1)} copy(bf16[256,2048]{1,0:T(8,128)(2,1)} %convolution_convert_fusion) | data formatting | bytes 2097152 | tf_op jit(solution)/shard_map/convert_element_type | solution.py:115
  38.2 23.6 %all-to-all-done.2 = bf16[32,256,64]{1,2,0:T(8,128)(2,1)} async-done(((bf16[32,256,64]{1,2,0:T(8,128)(2,1)}), bf16[32,256,64]{1,2,0:T(8,128)(2,1)}, u32[]{:S(2)}, u32[]{:S(2)}) %all-to-all-start.2) | async-done | bytes 1048608 | tf_op jit(solution)/shard_map/all_to_all | solution.py:30
  61.7 5.1 %all-to-all-start.1 = ((bf16[32,256,64]{1,2,0:T(8,128)(2,1)}), bf16[32,256,64]{1,2,0:T(8,128)(2,1)}, u32[]{:S(2)}, u32[]{:S(2)}) async-start(bf16[32,256,64]{1,2,0:T(8,128)(2,1)} %bitcast.21), calls=%async_computation.1 | async-start | bytes 2097152 | tf_op jit(solution)/shard_map/all_to_all | solution.py:73
  67.7 1.4 convert_reduce_fusion
  69.1 1.8 %fusion.2 = bf16[32,64,64]{2,1,0:T(8,128)(2,1)S(1)} fusion(f32[256,64]{0,1:T(8,128)S(1)} %fusion.13, f32[32,256]{1,0:T(8,128)S(1)} %fusion.8, f32[256,64]{0,1:T(8,128)S(1)} %convert_reduce_fusion), kind=kOutput, calls=%fused_computation.4 | convolution fusion | flops 403308544 | bytes 425984 | tf_op jit(solution)/shard_map/dot_general | solution.py:90
  71.4 2.9 %collective-permute-start.1 = (bf16[32,4096]{1,0:T(8,128)(2,1)S(1)}, bf16[32,4096]{1,0:T(8,128)(2,1)S(1)}, u32[]{:S(2)}, u32[]{:S(2)}) collective-permute-start(bf16[32,4096]{1,0:T(8,128)(2,1)S(1)} %convert_element_type.41), channel_id=1, source_target_pairs={{0,480},{32,0},{64,32},{96,64},{128,96},{160,128},{192,160},{224,1... | collective-permute-start | bytes 786440 | tf_op jit(solution)/shard_map/ppermute | solution.py:21
  74.3 20.2 %all-to-all-done.1 = bf16[32,256,64]{1,2,0:T(8,128)(2,1)} async-done(((bf16[32,256,64]{1,2,0:T(8,128)(2,1)}), bf16[32,256,64]{1,2,0:T(8,128)(2,1)}, u32[]{:S(2)}, u32[]{:S(2)}) %all-to-all-start.1) | async-done | bytes 1048608 | tf_op jit(solution)/shard_map/all_to_all | solution.py:73
  94.5 2.0 %reduce_sum.31 = bf16[256,64]{0,1:T(8,128)(2,1)} reduce(bf16[32,256,64]{1,2,0:T(8,128)(2,1)} %all-to-all-done.1, bf16[]{:T(256)} %constant.102.clone.1), dimensions={0}, to_apply=%region_2.3 | reduce | flops 507904 | bytes 1081346 | tf_op jit(solution)/shard_map/reduce_sum | solution.py:74
  96.5 0.5 broadcast_in_dim.7
  97.1 2.9 %collective-permute-start.3 = (bf16[32,4096]{1,0:T(8,128)(2,1)S(1)}, bf16[32,4096]{1,0:T(8,128)(2,1)S(1)}, u32[]{:S(2)}, u32[]{:S(2)}) collective-permute-start(bf16[32,4096]{1,0:T(8,128)(2,1)S(1)} %collective-permute-done.1), channel_id=1, source_target_pairs={{0,480},{32,0},{64,32},{96,64},{128,96},{160,128},{192,160},{224,1... | collective-permute-start | bytes 786440 | tf_op jit(solution)/shard_map/ppermute | solution.py:21
  100.1 4.0 %collective-permute-done.2 = bf16[32,4096]{1,0:T(8,128)(2,1)S(1)} collective-permute-done((bf16[32,4096]{1,0:T(8,128)(2,1)S(1)}, bf16[32,4096]{1,0:T(8,128)(2,1)S(1)}, u32[]{:S(2)}, u32[]{:S(2)}) %collective-permute-start.2) | collective-permute-done | bytes 262176 | tf_op jit(solution)/shard_map/ppermute | solution.py:18
  104.1 3.0 %collective-permute-start.5 = (bf16[32,4096]{1,0:T(8,128)(2,1)S(1)}, bf16[32,4096]{1,0:T(8,128)(2,1)S(1)}, u32[]{:S(2)}, u32[]{:S(2)}) collective-permute-start(bf16[32,4096]{1,0:T(8,128)(2,1)S(1)} %collective-permute-done.3), channel_id=1, source_target_pairs={{0,480},{32,0},{64,32},{96,64},{128,96},{160,128},{192,160},{224,1... | collective-permute-start | bytes 786440 | tf_op jit(solution)/shard_map/ppermute | solution.py:21
  107.1 4.0 %collective-permute-done.4 = bf16[32,4096]{1,0:T(8,128)(2,1)S(1)} collective-permute-done((bf16[32,4096]{1,0:T(8,128)(2,1)S(1)}, bf16[32,4096]{1,0:T(8,128)(2,1)S(1)}, u32[]{:S(2)}, u32[]{:S(2)}) %collective-permute-start.4) | collective-permute-done | bytes 262176 | tf_op jit(solution)/shard_map/ppermute | solution.py:18
  111.1 3.0 %collective-permute-start.7 = (bf16[32,4096]{1,0:T(8,128)(2,1)S(1)}, bf16[32,4096]{1,0:T(8,128)(2,1)S(1)}, u32[]{:S(2)}, u32[]{:S(2)}) collective-permute-start(bf16[32,4096]{1,0:T(8,128)(2,1)S(1)} %collective-permute-done.5), channel_id=1, source_target_pairs={{0,480},{32,0},{64,32},{96,64},{128,96},{160,128},{192,160},{224,1... | collective-permute-start | bytes 786440 | tf_op jit(solution)/shard_map/ppermute | solution.py:21
  114.1 4.0 %collective-permute-done.6 = bf16[32,4096]{1,0:T(8,128)(2,1)S(1)} collective-permute-done((bf16[32,4096]{1,0:T(8,128)(2,1)S(1)}, bf16[32,4096]{1,0:T(8,128)(2,1)S(1)}, u32[]{:S(2)}, u32[]{:S(2)}) %collective-permute-start.6) | collective-permute-done | bytes 262176 | tf_op jit(solution)/shard_map/ppermute | solution.py:18
  118.1 3.0 %collective-permute-start.9 = (bf16[32,4096]{1,0:T(8,128)(2,1)S(1)}, bf16[32,4096]{1,0:T(8,128)(2,1)S(1)}, u32[]{:S(2)}, u32[]{:S(2)}) collective-permute-start(bf16[32,4096]{1,0:T(8,128)(2,1)S(1)} %collective-permute-done.7), channel_id=1, source_target_pairs={{0,480},{32,0},{64,32},{96,64},{128,96},{160,128},{192,160},{224,1... | collective-permute-start | bytes 786440 | tf_op jit(solution)/shard_map/ppermute | solution.py:21
  121.1 4.0 %collective-permute-done.8 = bf16[32,4096]{1,0:T(8,128)(2,1)S(1)} collective-permute-done((bf16[32,4096]{1,0:T(8,128)(2,1)S(1)}, bf16[32,4096]{1,0:T(8,128)(2,1)S(1)}, u32[]{:S(2)}, u32[]{:S(2)}) %collective-permute-start.8) | collective-permute-done | bytes 262176 | tf_op jit(solution)/shard_map/ppermute | solution.py:18
  125.1 3.0 %collective-permute-start.11 = (bf16[32,4096]{1,0:T(8,128)(2,1)S(1)}, bf16[32,4096]{1,0:T(8,128)(2,1)S(1)}, u32[]{:S(2)}, u32[]{:S(2)}) collective-permute-start(bf16[32,4096]{1,0:T(8,128)(2,1)S(1)} %collective-permute-done.9), channel_id=1, source_target_pairs={{0,480},{32,0},{64,32},{96,64},{128,96},{160,128},{192,160},{224,1... | collective-permute-start | bytes 786440 | tf_op jit(solution)/shard_map/ppermute | solution.py:21
  128.1 4.0 %collective-permute-done.10 = bf16[32,4096]{1,0:T(8,128)(2,1)S(1)} collective-permute-done((bf16[32,4096]{1,0:T(8,128)(2,1)S(1)}, bf16[32,4096]{1,0:T(8,128)(2,1)S(1)}, u32[]{:S(2)}, u32[]{:S(2)}) %collective-permute-start.10) | collective-permute-done | bytes 262176 | tf_op jit(solution)/shard_map/ppermute | solution.py:18
  132.1 3.0 %collective-permute-start.13 = (bf16[32,4096]{1,0:T(8,128)(2,1)S(1)}, bf16[32,4096]{1,0:T(8,128)(2,1)S(1)}, u32[]{:S(2)}, u32[]{:S(2)}) collective-permute-start(bf16[32,4096]{1,0:T(8,128)(2,1)S(1)} %collective-permute-done.11), channel_id=1, source_target_pairs={{0,480},{32,0},{64,32},{96,64},{128,96},{160,128},{192,160},{224,1... | collective-permute-start | bytes 786440 | tf_op jit(solution)/shard_map/ppermute | solution.py:21
  135.1 4.0 %collective-permute-done.12 = bf16[32,4096]{1,0:T(8,128)(2,1)S(1)} collective-permute-done((bf16[32,4096]{1,0:T(8,128)(2,1)S(1)}, bf16[32,4096]{1,0:T(8,128)(2,1)S(1)}, u32[]{:S(2)}, u32[]{:S(2)}) %collective-permute-start.12) | collective-permute-done | bytes 262176 | tf_op jit(solution)/shard_map/ppermute | solution.py:18
  139.2 6.9 %collective-permute-done.14 = bf16[32,4096]{1,0:T(8,128)(2,1)S(1)} collective-permute-done((bf16[32,4096]{1,0:T(8,128)(2,1)S(1)}, bf16[32,4096]{1,0:T(8,128)(2,1)S(1)}, u32[]{:S(2)}, u32[]{:S(2)}) %collective-permute-start.14) | collective-permute-done | bytes 262176 | tf_op jit(solution)/shard_map/ppermute | solution.py:18
  146.2 2.1 %convolution_multiply_fusion = f32[512,256]{1,0:T(8,128)} fusion(bf16[512,4096]{1,0:T(8,128)(2,1)S(1)} %constant_dynamic-update-slice_fusion, bf16[256,4096]{1,0:T(8,128)(2,1)S(1)} %copy-done), kind=kOutput, calls=%fused_computation.5 | convolution fusion | flops 1073872896 | bytes 6815744 | tf_op jit(solution)/shard_map/dot_general | solution.py:125
  (74 shorter events, 1.9 us)
Async XLA Ops:
  0.6 145.5 %copy-start = (bf16[256,4096]{1,0:T(8,128)(2,1)S(1)}, bf16[256,4096]{1,0:T(8,128)(2,1)}, u32[]{:S(2)}) copy-start(bf16[256,4096]{1,0:T(8,128)(2,1)} %param.15) | copy-start | bytes 6291460
  0.6 33.6 %copy-start.1 = (bf16[2048,256]{1,0:T(8,128)(2,1)S(1)}, bf16[2048,256]{1,0:T(8,128)(2,1)}, u32[]{:S(2)}) copy-start(bf16[2048,256]{1,0:T(8,128)(2,1)} %param.9) | copy-start | bytes 3145732
  0.7 33.6 %copy-start.4 = (s32[256]{0:T(256)S(1)}, s32[256]{0:T(256)}, u32[]{:S(2)}) copy-start(s32[256]{0:T(256)} %param.12) | copy-start | bytes 3076
  3.6 23.2 %all-to-all-start = ((f32[32,2,256]{2,1,0:T(2,128)}), f32[32,2,256]{2,1,0:T(2,128)S(1)}, u32[]{:S(2)}, u32[]{:S(2)}) async-start(f32[32,2,256]{2,1,0:T(2,128)} %broadcast_in_dim.6), calls=%async_computation | async-start | bytes 131072 | tf_op jit(solution)/shard_map/all_to_all | solution.py:30
  29.4 37.8 %copy-start.5 = (s32[256]{0:T(256)S(1)}, s32[256]{0:T(256)}, u32[]{:S(2)}) copy-start(s32[256]{0:T(256)} %param.14) | copy-start | bytes 3076
  29.4 32.3 %all-to-all-start.2 = ((bf16[32,256,64]{1,2,0:T(8,128)(2,1)}), bf16[32,256,64]{1,2,0:T(8,128)(2,1)}, u32[]{:S(2)}, u32[]{:S(2)}) async-start(bf16[32,256,64]{1,2,0:T(8,128)(2,1)} %broadcast_in_dim.8), calls=%async_computation.2 | async-start | bytes 2097152 | tf_op jit(solution)/shard_map/all_to_all | solution.py:30
  35.8 31.4 %copy-start.2 = (bf16[256,2048]{1,0:T(8,128)(2,1)S(1)}, bf16[256,2048]{1,0:T(8,128)(2,1)}, u32[]{:S(2)}) copy-start(bf16[256,2048]{1,0:T(8,128)(2,1)} %param.8) | copy-start | bytes 3145732
  35.8 31.5 %copy-start.3 = (bf16[2048,64]{0,1:T(8,128)(2,1)S(1)}, bf16[2048,64]{0,1:T(8,128)(2,1)}, u32[]{:S(2)}) copy-start(bf16[2048,64]{0,1:T(8,128)(2,1)} %param.10) | copy-start | bytes 786436
  61.7 32.8 %all-to-all-start.1 = ((bf16[32,256,64]{1,2,0:T(8,128)(2,1)}), bf16[32,256,64]{1,2,0:T(8,128)(2,1)}, u32[]{:S(2)}, u32[]{:S(2)}) async-start(bf16[32,256,64]{1,2,0:T(8,128)(2,1)} %bitcast.21), calls=%async_computation.1 | async-start | bytes 2097152 | tf_op jit(solution)/shard_map/all_to_all | solution.py:73
  71.3 25.7 %collective-permute-start = (bf16[32,4096]{1,0:T(8,128)(2,1)S(1)}, bf16[32,4096]{1,0:T(8,128)(2,1)S(1)}, u32[]{:S(2)}, u32[]{:S(2)}) collective-permute-start(bf16[32,4096]{1,0:T(8,128)(2,1)S(1)} %convert_element_type.41), channel_id=1, source_target_pairs={{0,32},{32,64},{64,96},{96,128},{128,160},{160,192},{192,224},{224... | collective-permute-start | bytes 786440 | tf_op jit(solution)/shard_map/ppermute | solution.py:18
  71.4 25.7 %collective-permute-start.1 = (bf16[32,4096]{1,0:T(8,128)(2,1)S(1)}, bf16[32,4096]{1,0:T(8,128)(2,1)S(1)}, u32[]{:S(2)}, u32[]{:S(2)}) collective-permute-start(bf16[32,4096]{1,0:T(8,128)(2,1)S(1)} %convert_element_type.41), channel_id=1, source_target_pairs={{0,480},{32,0},{64,32},{96,64},{128,96},{160,128},{192,160},{224,1... | collective-permute-start | bytes 786440 | tf_op jit(solution)/shard_map/ppermute | solution.py:21
  97.0 7.0 %collective-permute-start.2 = (bf16[32,4096]{1,0:T(8,128)(2,1)S(1)}, bf16[32,4096]{1,0:T(8,128)(2,1)S(1)}, u32[]{:S(2)}, u32[]{:S(2)}) collective-permute-start(bf16[32,4096]{1,0:T(8,128)(2,1)S(1)} %collective-permute-done), channel_id=1, source_target_pairs={{0,32},{32,64},{64,96},{96,128},{128,160},{160,192},{192,224},{224... | collective-permute-start | bytes 786440 | tf_op jit(solution)/shard_map/ppermute | solution.py:18
  97.1 7.0 %collective-permute-start.3 = (bf16[32,4096]{1,0:T(8,128)(2,1)S(1)}, bf16[32,4096]{1,0:T(8,128)(2,1)S(1)}, u32[]{:S(2)}, u32[]{:S(2)}) collective-permute-start(bf16[32,4096]{1,0:T(8,128)(2,1)S(1)} %collective-permute-done.1), channel_id=1, source_target_pairs={{0,480},{32,0},{64,32},{96,64},{128,96},{160,128},{192,160},{224,1... | collective-permute-start | bytes 786440 | tf_op jit(solution)/shard_map/ppermute | solution.py:21
  104.1 7.0 %collective-permute-start.4 = (bf16[32,4096]{1,0:T(8,128)(2,1)S(1)}, bf16[32,4096]{1,0:T(8,128)(2,1)S(1)}, u32[]{:S(2)}, u32[]{:S(2)}) collective-permute-start(bf16[32,4096]{1,0:T(8,128)(2,1)S(1)} %collective-permute-done.2), channel_id=1, source_target_pairs={{0,32},{32,64},{64,96},{96,128},{128,160},{160,192},{192,224},{224... | collective-permute-start | bytes 786440 | tf_op jit(solution)/shard_map/ppermute | solution.py:18
  104.1 7.0 %collective-permute-start.5 = (bf16[32,4096]{1,0:T(8,128)(2,1)S(1)}, bf16[32,4096]{1,0:T(8,128)(2,1)S(1)}, u32[]{:S(2)}, u32[]{:S(2)}) collective-permute-start(bf16[32,4096]{1,0:T(8,128)(2,1)S(1)} %collective-permute-done.3), channel_id=1, source_target_pairs={{0,480},{32,0},{64,32},{96,64},{128,96},{160,128},{192,160},{224,1... | collective-permute-start | bytes 786440 | tf_op jit(solution)/shard_map/ppermute | solution.py:21
  111.1 7.0 %collective-permute-start.6 = (bf16[32,4096]{1,0:T(8,128)(2,1)S(1)}, bf16[32,4096]{1,0:T(8,128)(2,1)S(1)}, u32[]{:S(2)}, u32[]{:S(2)}) collective-permute-start(bf16[32,4096]{1,0:T(8,128)(2,1)S(1)} %collective-permute-done.4), channel_id=1, source_target_pairs={{0,32},{32,64},{64,96},{96,128},{128,160},{160,192},{192,224},{224... | collective-permute-start | bytes 786440 | tf_op jit(solution)/shard_map/ppermute | solution.py:18
  111.1 7.0 %collective-permute-start.7 = (bf16[32,4096]{1,0:T(8,128)(2,1)S(1)}, bf16[32,4096]{1,0:T(8,128)(2,1)S(1)}, u32[]{:S(2)}, u32[]{:S(2)}) collective-permute-start(bf16[32,4096]{1,0:T(8,128)(2,1)S(1)} %collective-permute-done.5), channel_id=1, source_target_pairs={{0,480},{32,0},{64,32},{96,64},{128,96},{160,128},{192,160},{224,1... | collective-permute-start | bytes 786440 | tf_op jit(solution)/shard_map/ppermute | solution.py:21
  118.1 7.0 %collective-permute-start.8 = (bf16[32,4096]{1,0:T(8,128)(2,1)S(1)}, bf16[32,4096]{1,0:T(8,128)(2,1)S(1)}, u32[]{:S(2)}, u32[]{:S(2)}) collective-permute-start(bf16[32,4096]{1,0:T(8,128)(2,1)S(1)} %collective-permute-done.6), channel_id=1, source_target_pairs={{0,32},{32,64},{64,96},{96,128},{128,160},{160,192},{192,224},{224... | collective-permute-start | bytes 786440 | tf_op jit(solution)/shard_map/ppermute | solution.py:18
  118.1 7.0 %collective-permute-start.9 = (bf16[32,4096]{1,0:T(8,128)(2,1)S(1)}, bf16[32,4096]{1,0:T(8,128)(2,1)S(1)}, u32[]{:S(2)}, u32[]{:S(2)}) collective-permute-start(bf16[32,4096]{1,0:T(8,128)(2,1)S(1)} %collective-permute-done.7), channel_id=1, source_target_pairs={{0,480},{32,0},{64,32},{96,64},{128,96},{160,128},{192,160},{224,1... | collective-permute-start | bytes 786440 | tf_op jit(solution)/shard_map/ppermute | solution.py:21
  125.1 7.0 %collective-permute-start.10 = (bf16[32,4096]{1,0:T(8,128)(2,1)S(1)}, bf16[32,4096]{1,0:T(8,128)(2,1)S(1)}, u32[]{:S(2)}, u32[]{:S(2)}) collective-permute-start(bf16[32,4096]{1,0:T(8,128)(2,1)S(1)} %collective-permute-done.8), channel_id=1, source_target_pairs={{0,32},{32,64},{64,96},{96,128},{128,160},{160,192},{192,224},{224... | collective-permute-start | bytes 786440 | tf_op jit(solution)/shard_map/ppermute | solution.py:18
  125.1 7.0 %collective-permute-start.11 = (bf16[32,4096]{1,0:T(8,128)(2,1)S(1)}, bf16[32,4096]{1,0:T(8,128)(2,1)S(1)}, u32[]{:S(2)}, u32[]{:S(2)}) collective-permute-start(bf16[32,4096]{1,0:T(8,128)(2,1)S(1)} %collective-permute-done.9), channel_id=1, source_target_pairs={{0,480},{32,0},{64,32},{96,64},{128,96},{160,128},{192,160},{224,1... | collective-permute-start | bytes 786440 | tf_op jit(solution)/shard_map/ppermute | solution.py:21
  132.1 7.0 %collective-permute-start.12 = (bf16[32,4096]{1,0:T(8,128)(2,1)S(1)}, bf16[32,4096]{1,0:T(8,128)(2,1)S(1)}, u32[]{:S(2)}, u32[]{:S(2)}) collective-permute-start(bf16[32,4096]{1,0:T(8,128)(2,1)S(1)} %collective-permute-done.10), channel_id=1, source_target_pairs={{0,32},{32,64},{64,96},{96,128},{128,160},{160,192},{192,224},{224... | collective-permute-start | bytes 786440 | tf_op jit(solution)/shard_map/ppermute | solution.py:18
  132.1 7.0 %collective-permute-start.13 = (bf16[32,4096]{1,0:T(8,128)(2,1)S(1)}, bf16[32,4096]{1,0:T(8,128)(2,1)S(1)}, u32[]{:S(2)}, u32[]{:S(2)}) collective-permute-start(bf16[32,4096]{1,0:T(8,128)(2,1)S(1)} %collective-permute-done.11), channel_id=1, source_target_pairs={{0,480},{32,0},{64,32},{96,64},{128,96},{160,128},{192,160},{224,1... | collective-permute-start | bytes 786440 | tf_op jit(solution)/shard_map/ppermute | solution.py:21
  139.1 7.0 %collective-permute-start.14 = (bf16[32,4096]{1,0:T(8,128)(2,1)S(1)}, bf16[32,4096]{1,0:T(8,128)(2,1)S(1)}, u32[]{:S(2)}, u32[]{:S(2)}) collective-permute-start(bf16[32,4096]{1,0:T(8,128)(2,1)S(1)} %collective-permute-done.12), channel_id=1, source_target_pairs={{0,32},{32,64},{64,96},{96,128},{128,160},{160,192},{192,224},{224... | collective-permute-start | bytes 786440 | tf_op jit(solution)/shard_map/ppermute | solution.py:18
